TPU v7x, 128 devices: a whole 4x4x4 slice. The times are simulated.
128 devices in a mesh: slab: 16 (over x, z), chan: 8 (over y, core).
Axes of the slice: x: 4, y: 4, z: 4, core: 2. Of those that a mesh axis runs over, the one named last changes fastest.
Arguments:
- stream_speed_field: bfloat16 [3, 8, 8, 8, 65536], P(None, None, None, None, ('slab', 'chan')), may hold values from -6 to 6
- liquid_to_solid_element: int32 [65536], P(('slab', 'chan')), may hold values from 0 to 65535, as said below
- previous_panel_warmth: float32 [8, 8, 8, 16, 4096], P(None, None, None, 'chan', 'slab'), may hold values from -6 to 6
- pointwise_energy_source: float32 [8, 8, 8, 16, 4096], P(None, None, None, 'chan', 'slab'), may hold values from -6 to 6
- coked_element_flags: int32 [16, 4096], P('chan', 'slab'), may hold values from 0 to 1, as said below
- coking_thickness_plies: int32 [16, 4096], P('chan', 'slab'), may hold values from 1 to 8
Outputs:
- stepped_stream_speed: bfloat16 [3, 8, 8, 8, 65536], P(None, None, None, None, ('slab', 'chan'))
- solved_panel_warmth: float32 [8, 8, 8, 16, 4096], P(None, None, None, 'chan', 'slab')
Inputs may be any that keep to these rules, and one draw needn't show every extreme that they name: `liquid_to_solid_element`: A permutation of the element numbers. Element n belongs to thermal device n // 512 (devices numbered slab first, then chan) at local position n % 512. The fluid device f holds 256 elements of thermal device f and at most 128 of each of the thermal devices f + 1, f - 1 and f + 8 (modulo the number of devices), none of any other; these three counts are the same for every f, and one of them is 128. `coked_element_flags`: at most 192 flagged elements among one thermal device's elements, and exactly 192 on some device.
All inputs are finite; a program needn't handle non-finite values.
Results may differ from a plain program's by a relative error of at most 0.005.
Values may be sent and summed in bfloat16 or wider, within the bound.
A program may use at most 128 MiB of HBM per device.

v0:
```python
import functools

import jax
import jax.numpy as jnp
import numpy as np
from jax import lax
from jax.experimental import pallas as pl
from jax.experimental.pallas import tpu as pltpu
from jax.sharding import PartitionSpec as P

F32 = jnp.float32
BF16 = jnp.bfloat16
MESH = pl.DeviceIdType.MESH
ITERS = 5
SCALE = 64.0
NT = (((1,), (1,)), ((), ()))
NN = (((1,), (0,)), ((), ()))


def gll():
    points = np.array(
        [
            -1.0,
            -0.8717401485096066,
            -0.5917001814331423,
            -0.2092992179024789,
            0.2092992179024789,
            0.5917001814331423,
            0.8717401485096066,
            1.0,
        ]
    )
    weights = np.array(
        [
            1.0 / 28.0,
            0.2107042271435061,
            0.3411226924835044,
            0.4124587946587038,
            0.4124587946587038,
            0.3411226924835044,
            0.2107042271435061,
            1.0 / 28.0,
        ]
    )
    low = np.ones(8)
    high = points.copy()
    for degree in range(1, 7):
        low, high = high, ((2 * degree + 1) * points * high - degree * low) / (degree + 1)
    gaps = points[:, None] - points[None, :] + np.eye(8)
    deriv = high[:, None] / (high[None, :] * gaps)
    deriv = deriv * (1.0 - np.eye(8))
    deriv[0, 0] = -14.0
    deriv[7, 7] = 14.0
    return deriv, weights


def two(matrix):
    high = np.asarray(matrix, np.float32).astype(BF16).astype(np.float64)
    return high, matrix - high


def operators():
    deriv, weights = gll()
    second = deriv @ deriv
    eye = np.eye
    kron = np.kron
    along_s = kron(eye(4), kron(deriv, eye(8)))
    along_t = kron(eye(32), deriv)
    along_r = kron(deriv, eye(32))
    ds_hi, ds_lo = two(along_s)
    dt_hi, dt_lo = two(along_t)
    forward = np.block([[ds_hi, ds_lo], [dt_hi, dt_lo]])
    backward = np.block([[ds_hi.T, dt_hi.T, ds_lo.T, dt_lo.T]])
    lap_st = 0.0002 * (kron(eye(4), kron(second, eye(8))) + kron(eye(32), second))
    both_r = np.block([[along_r], [0.0002 * kron(second, eye(32))]])
    volume = (weights[:, None, None] * weights[None, :, None] * weights[None, None, :]).reshape(512, 1)
    cast = lambda m: jnp.asarray(np.asarray(m, np.float32).astype(BF16))
    return {
        "forward": cast(forward),
        "backward": cast(backward),
        "lap_st": cast(lap_st),
        "both_r": cast(both_r),
        "volume": jnp.asarray(np.broadcast_to(volume, (512, 128)), F32),
    }


def dot(a, b, dims=NN):
    return lax.dot_general(a, b, dims, preferred_element_type=F32)


def iota(shape, dim):
    return lax.broadcasted_iota(jnp.int32, shape, dim)


def krylov_weights(m):
    n = ITERS
    zero = jnp.zeros_like(m[0])
    older, newer = [zero] * (2 * n), list(m)
    diag = [newer[1] / newer[0]]
    off = [zero]
    for k in range(1, n):
        fresh = [zero] * (2 * n)
        for l in range(k, 2 * n - k):
            fresh[l] = newer[l + 1] - diag[k - 1] * newer[l] - off[k - 1] * older[l]
        diag.append(fresh[k + 1] / fresh[k] - newer[k] / newer[k - 1])
        off.append(fresh[k] / newer[k - 1])
        older, newer = newer, fresh
    alpha = [1.0 / diag[0]]
    beta = []
    for k in range(1, n):
        beta.append(off[k] * alpha[k - 1] * alpha[k - 1])
        alpha.append(1.0 / (diag[k] - beta[k - 1] / alpha[k - 1]))
    one = jnp.ones_like(zero)
    res, way, sol = [one], [one], [zero] * n
    for k in range(n):
        for i in range(k + 1):
            sol[i] = sol[i] + alpha[k] * way[i]
        if k < n - 1:
            res = res + [zero]
            for i in range(k + 1):
                res[i + 1] = res[i + 1] - alpha[k] * way[i]
            way = [res[i] + (beta[k] * way[i] if i <= k else 0.0) for i in range(k + 2)]
    return sol


EDGES = ((1, 0), (-1, 0), (1, 1), (1, -1), (-1, 1), (-1, -1))
HALO = EDGES + ((0, 1), (0, -1))


def along(matrix, v):
    even = [v[k] + v[7 - k] for k in range(4)]
    odd = [v[k] - v[7 - k] for k in range(4)]
    first, last = [], []
    for i in range(4):
        same = [0.5 * float(matrix[i, k] + matrix[i, 7 - k]) for k in range(4)]
        flip = [0.5 * float(matrix[i, k] - matrix[i, 7 - k]) for k in range(4)]
        p = (same[0] * even[0] + same[1] * even[1]) + (same[2] * even[2] + same[3] * even[3])
        q = (flip[0] * odd[0] + flip[1] * odd[1]) + (flip[2] * odd[2] + flip[3] * odd[3])
        first.append(p + q)
        last.append(q - p)
    return first + last[::-1]


def cut(x):
    high = x.astype(BF16)
    return high, (x - high.astype(F32)).astype(BF16)


def ends_middle(low, high):
    half = iota(low.shape, 1) < 64
    return jnp.where(half, low, high), jnp.where(half, high, low)


def kernel(
    n_slab,
    n_chan,
    u_hbm,
    index_hbm,
    prev_hbm,
    source_hbm,
    flag_hbm,
    ply_hbm,
    forward_hbm,
    backward_hbm,
    lap_hbm,
    both_hbm,
    volume_hbm,
    new_ref,
    out_ref,
    u_ref,
    index_ref,
    prev_ref,
    source_ref,
    flag_ref,
    ply_ref,
    fwd_st,
    bwd_st,
    lap_st,
    both_r,
    volume_ref,
    speed_grad,
    lap,
    cond,
    own_pack,
    put_pack,
    got_pack,
    basis,
    kap,
    mix_ref,
    inv_mult,
    grad,
    ysum,
    flux,
    acc,
    edge_out,
    edge_in,
    side_out,
    side_in,
    chan_sum,
    slab_sum,
    load_sem,
    pack_send,
    pack_recv,
    halo_send,
    halo_recv,
    chan_send,
    chan_recv,
    slab_send,
    slab_recv,
):
    slab = lax.axis_index("slab")
    chan = lax.axis_index("chan")
    device = slab * n_chan + chan
    devices = n_slab * n_chan

    def near(ds, dc):
        return (lax.rem(slab + ds + n_slab, n_slab), lax.rem(chan + dc + n_chan, n_chan))

    left, right = pl.ds(0, 256), pl.ds(256, 256)
    loads = [
        pltpu.make_async_copy(src, dst, load_sem.at[k])
        for k, (src, dst) in enumerate(
            (
                (prev_hbm, prev_ref),
                (source_hbm, source_ref),
                (volume_hbm, volume_ref),
                (flag_hbm, flag_ref),
                (ply_hbm, ply_ref),
                (u_hbm.at[:, :, left], u_ref.at[:, :, left]),
                (lap_hbm, lap_st),
                (both_hbm, both_r),
                (forward_hbm, fwd_st.at[:, pl.ds(0, 512)]),
                (u_hbm.at[:, :, right], u_ref.at[:, :, right]),
                (forward_hbm.at[:, pl.ds(0, 256)], fwd_st.at[:, pl.ds(512, 256)]),
                (backward_hbm, bwd_st.at[:, pl.ds(0, 1024)]),
                (backward_hbm.at[:, pl.ds(0, 512)], bwd_st.at[:, pl.ds(1024, 512)]),
                (index_hbm, index_ref),
            )
        )
    ]
    loads[13].start()
    for load in loads[:13]:
        load.start()

    barrier = pltpu.get_barrier_semaphore()
    greet = [near(*d) for d in HALO]
    greet += [(slab, lax.rem(chan + j, n_chan)) for j in range(2, n_chan - 1)]
    greet += [(lax.rem(slab + j, n_slab), chan) for j in range(2, n_slab - 1)]
    for peer in greet:
        pl.semaphore_signal(barrier, inc=1, device_id=peer, device_id_type=MESH)

    loads[13].wait()
    target = index_ref[...]
    slot = target & 511
    distance = ((target >> 9) - device) & (devices - 1)
    group = jnp.where(
        distance == 1,
        1,
        jnp.where(distance == devices - 1, 2, jnp.where(distance == n_chan, 3, 0)),
    )
    member = iota((8, 512), 0) == group
    before = (iota((512, 512), 0) < iota((512, 512), 1)).astype(F32).astype(BF16)
    rank = dot(member.astype(F32).astype(BF16), before)
    begin = jnp.where(iota((8, 512), 0) == 0, 0, 128 + 128 * iota((8, 512), 0)).astype(F32)
    position = jnp.sum(jnp.where(member, rank + begin, 0.0), axis=0, keepdims=True).astype(jnp.int32)
    code = jnp.where(
        iota((16, 512), 0) == 0,
        (slot >> 5) + 1,
        jnp.where(iota((16, 512), 0) == 1, slot & 31, 0),
    )
    cond[512:528] = code.astype(F32).astype(BF16)

    for load in loads[:5]:
        load.wait()
    for l in range(2):
        halves = []
        for h in range(2):
            rows = pl.ds(2 * h + l, 512, stride=4)
            halves.append(volume_ref[...] * (0.05 * prev_ref[rows, :] + source_ref[rows, :]))
        for m, value in enumerate(ends_middle(*halves)):
            basis[0, :, :, :, pl.ds(256 * m + 128 * l, 128)] = value.reshape(8, 8, 8, 128)
    damping = []
    mixing = []
    for l in range(2):
        flag = flag_ref[pl.ds(l, 1)]
        ply = ply_ref[pl.ds(l, 1)].astype(F32)
        damp = jnp.where(flag == 1, 1.0 / (1.0 + 0.25 * ply), 1.0) * (1.0 / SCALE)
        mix = 0.4 * flag.astype(F32) * ply / (ply + 1.0)
        wide = [jnp.broadcast_to(x, (8, 256)) for x in (damp, mix)]
        damping.append(ends_middle(wide[0][:, :128], wide[0][:, 128:]))
        mixing.append(ends_middle(wide[1][:, :128], wide[1][:, 128:]))
    damping = [damping[l][m][0:1] for m in range(2) for l in range(2)]
    mixing = [mixing[l][m] for m in range(2) for l in range(2)]
    for tile in range(4):
        mix_ref[:, pl.ds(128 * tile, 128)] = mixing[tile]

    def fluid(block):
        lane = pl.ds(256 * block, 256)
        for c in range(3):
            flat = u_ref[pl.ds(64 * c, 64), :, lane].astype(F32).reshape(512, 256)
            low = flat.astype(BF16)
            for h in range(2):
                rows = pl.ds(256 * h, 256)
                part = low[256 * h : 256 * h + 256]
                both = dot(fwd_st[:, 0:256], part)
                speed_grad[c, 1, rows, lane] = both[:256]
                speed_grad[c, 2, rows, lane] = both[256:]
                lap[c, rows, lane] = dot(lap_st[...], part)
            by_r = flat.reshape(8, 64, 256)
            for q in range(2):
                part = by_r[:, 32 * q : 32 * q + 32].reshape(256, 256).astype(BF16)
                both = dot(both_r[...], part).reshape(16, 32, 256)
                for r in range(8):
                    rows = pl.ds(64 * r + 32 * q, 32)
                    speed_grad[c, 0, rows, lane] = both[r]
                    lap[c, rows, lane] += both[8 + r]
            for n in range(32):
                for tile in range(2):
                    part = pl.ds(256 * block + 128 * tile, 128)
                    rows = pl.ds(16 * n, 16)
                    u = [u_ref[pl.ds(64 * k + 2 * n, 2), :, part].astype(F32).reshape(16, 128) for k in range(3)]
                    turn = (
                        u[0] * speed_grad[c, 0, rows, part]
                        + u[1] * speed_grad[c, 1, rows, part]
                        + u[2] * speed_grad[c, 2, rows, part]
                    )
                    new = ((u[c] + lap[c, rows, part]) - 0.01 * turn).astype(BF16).astype(F32)
                    new_ref[pl.ds(64 * c + 2 * n, 2), :, part] = new.reshape(2, 8, 128).astype(BF16)
                    square = new * new if c == 0 else ysum[rows, part] + new * new
                    if c < 2:
                        ysum[rows, part] = square
                    else:
                        cond[rows, part] = (1.0 + 0.5 * square).astype(BF16)

    for load in loads[5:9]:
        load.wait()
    fluid(0)

    lane8 = iota((8, 128), 1)
    has_left = slab > 0
    has_right = slab < n_slab - 1
    has_under = chan > 0
    has_over = chan < n_chan - 1
    has_next = {(1, 0): has_right, (-1, 0): has_left, (0, 1): has_over, (0, -1): has_under}

    def both_of(ds, dc):
        if ds == 0 or dc == 0:
            return has_next[ds, dc]
        return has_next[ds, 0] & has_next[0, dc]

    SIDES = ((0, 1, 0), (0, -1, 0), (0, 1, 1), (0, -1, 1))

    def halo_copies(i, want_edges, want_sides):
        turn = i % 2 if isinstance(i, int) else lax.rem(i, 2)

        def remote(src, dst, number, ds, dc):
            return pltpu.make_async_remote_copy(
                src_ref=src,
                dst_ref=dst,
                send_sem=halo_send.at[turn, number],
                recv_sem=halo_recv.at[turn, number],
                device_id=near(ds, dc),
                device_id_type=MESH,
            )

        edges = [
            (ds, dc, remote(edge_out.at[turn, 0 if ds == 1 else 1], edge_in.at[turn, d], d, ds, dc))
            for d, (ds, dc) in enumerate(EDGES)
            if want_edges
        ]
        sides = []
        for d, (ds, dc, m) in enumerate(SIDES):
            if m not in want_sides:
                continue
            k = 0 if dc == 1 else 1
            sides.append((ds, dc, remote(side_out.at[turn, k, m], side_in.at[turn, k, m], 6 + d, ds, dc)))
        return turn, edges, sides

    def send(copies):
        for ds, dc, copy in copies:
            pl.when(both_of(ds, dc))(copy.start)

    def arrive(copies):
        for ds, dc, copy in copies:
            pl.when(both_of(ds, dc))(copy.wait_send)
            pl.when(both_of(-ds, -dc))(copy.wait_recv)

    def lanes(m, l):
        return pl.ds(256 * m + 128 * l, 128)

    def between(i, m, turn):
        side_out[turn, 0, m] = basis[i, :, 7, :, lanes(m, 1)]
        side_out[turn, 1, m] = basis[i, :, 0, :, lanes(m, 0)]
        both = basis[i, :, 7, :, lanes(m, 0)] + basis[i, :, 0, :, lanes(m, 1)]
        basis[i, :, 7, :, lanes(m, 0)] = both
        basis[i, :, 0, :, lanes(m, 1)] = both

    def start_ends(i):
        turn, edges, sides = halo_copies(i, True, (0,))
        between(i, 0, turn)
        up = jnp.zeros((8, 128), F32)
        down = jnp.zeros((8, 128), F32)
        for l in range(2):
            for s in range(8):
                to = s + 8 * l
                here = lane8 == to
                up = jnp.where(here, pltpu.roll(basis[i, 7, s, :, lanes(0, l)], (to - 127) % 128, 1), up)
                down = jnp.where(here, pltpu.roll(basis[i, 0, s, :, lanes(0, l)], to, 1), down)
        edge_out[turn, 0] = up
        edge_out[turn, 1] = down
        send(edges)
        send(sides)

    def start_middle(i):
        turn, edges, sides = halo_copies(i, False, (1,))
        between(i, 1, turn)
        send(sides)

    def finish_sides(i):
        turn, edges, sides = halo_copies(i, False, (0, 1))
        arrive(sides)
        for k, (has, s, l) in enumerate(((has_under, 0, 0), (has_over, 7, 1))):
            for m in range(2):
                basis[i, :, s, :, lanes(m, l)] += jnp.where(has, side_in[turn, k, m], 0.0)
        j = iota((64, 128), 1)
        for l in range(2):
            high = [basis[i, 7, :, :, lanes(m, l)].reshape(64, 128) for m in range(2)]
            low = [basis[i, 0, :, :, lanes(m, l)].reshape(64, 128) for m in range(2)]
            ahead = [pltpu.roll(x, 127, 1) for x in low]
            behind = [pltpu.roll(x, 1, 1) for x in high]
            for m in range(2):
                more = jnp.where(j == 63, ahead[1 - m], ahead[m])
                less = jnp.where(j == 64, behind[1 - m], behind[m])
                if m == 0:
                    more = jnp.where(j == 127, 0.0, more)
                    less = jnp.where(j == 0, 0.0, less)
                basis[i, 7, :, :, lanes(m, l)] = (high[m] + more).reshape(8, 8, 128)
                basis[i, 0, :, :, lanes(m, l)] = (low[m] + less).reshape(8, 8, 128)

    def finish_edges(i):
        turn, edges, sides = halo_copies(i, True, ())
        arrive(edges)
        first = lane8 == 0
        last = lane8 == 127

        def add(l, s, at, slot_left, slot_right, has):
            left_ok = has_left if has is None else has_left & has
            right_ok = has_right if has is None else has_right & has
            basis[i, 0, s, :, lanes(0, l)] += jnp.where(
                first & left_ok, pltpu.roll(edge_in[turn, slot_left], (128 - at) % 128, 1), 0.0
            )
            basis[i, 7, s, :, lanes(0, l)] += jnp.where(
                last & right_ok, pltpu.roll(edge_in[turn, slot_right], (127 - at) % 128, 1), 0.0
            )

        for l in range(2):
            for s in range(8):
                add(l, s, s + 8 * l, EDGES.index((1, 0)), EDGES.index((-1, 0)), None)
        add(0, 0, 15, EDGES.index((1, 1)), EDGES.index((-1, 1)), has_under)
        add(1, 7, 0, EDGES.index((1, -1)), EDGES.index((-1, -1)), has_over)

    loads[9].wait()
    fluid(1)
    pl.semaphore_wait(barrier, len(greet))
    start_ends(0)
    start_middle(0)

    def packed(start, count):
        chosen = (iota((count, 512), 0) + start == position).astype(F32).astype(BF16)
        return dot(cond[...], chosen, NT).astype(BF16)

    def device_at(step):
        number = lax.rem(device + step + devices, devices)
        return (number // n_chan, lax.rem(number, n_chan))

    moves = [
        pltpu.make_async_remote_copy(
            src_ref=put_pack.at[k],
            dst_ref=got_pack.at[k],
            send_sem=pack_send.at[k],
            recv_sem=pack_recv.at[k],
            device_id=device_at(step),
            device_id_type=MESH,
        )
        for k, step in enumerate((n_chan, 1, -1))
    ]
    late = packed(512, 128)
    put_pack[0] = late
    moves[0].start()
    soon = packed(256, 256)
    put_pack[1] = soon[:, :128]
    put_pack[2] = soon[:, 128:]
    moves[1].start()
    moves[2].start()
    own_pack[...] = packed(0, 256)

    def place(block):
        code = block[512:528].astype(F32)
        slot = ((code[0:1] - 1.0) * 32.0 + code[1:2]).astype(jnp.int32)
        lane = iota((512, block.shape[1]), 0)
        here = lane & 127
        axial = here + jnp.where((lane < 256) == (here < 64), 0, 128)
        chosen = (((lane >> 7) & 1) * 256 + axial == slot).astype(F32).astype(BF16)
        return dot(block[0:512], chosen, NT)

    kap[...] = place(own_pack[...])
    node = iota((512, 128), 0)
    at_r = node >> 6
    at_s = (node >> 3) & 7
    for m in range(2):
        for l in range(2):
            here = iota((512, 128), 1)
            axial = slab * 256 + here + jnp.where(here < 64, 128 * m, 128 - 128 * m)
            m_r = jnp.where(((at_r == 0) & (axial > 0)) | ((at_r == 7) & (axial < n_slab * 256 - 1)), 0.5, 1.0)
            lateral = chan * 2 + l
            m_s = jnp.where(((at_s == 0) & (lateral > 0)) | ((at_s == 7) & (lateral < n_chan * 2 - 1)), 0.5, 1.0)
            inv_mult[:, lanes(m, l)] = m_r * m_s

    deriv = gll()[0]

    spare = lax.div(slab, n_slab)

    def gradient(i, block):
        lane = pl.ds(256 * block, 256)
        pairs = [cut(basis[i, 4 * h : 4 * h + 4, :, :, lane].reshape(256, 256)) for h in range(2)]

        def turn(h):
            high, low = pairs[h]
            both = dot(fwd_st[...], jnp.concatenate([high, high, low], 0))
            grad[1, pl.ds(256 * h, 256), lane] = both[:256]
            grad[2, pl.ds(256 * h, 256), lane] = both[256:]
            return both

        basis[ITERS + spare, 0, 0, :, 0:128] = turn(0)[0:8, 0:128]
        for s in range(8):
            for tile in range(2):
                part = pl.ds(256 * block + 128 * tile, 128)
                out = along(deriv, [basis[i, r, s, :, part] for r in range(8)])
                for r in range(8):
                    grad[0, pl.ds(64 * r + 8 * s, 8), part] = out[r]
        turn(1)

    def fold(x):
        total = jnp.sum(x.reshape(x.shape[0] // 8, 8, 256), axis=0)
        return total[:, :128] + total[:, 128:]

    def norm(i):
        totals = [None] * 4
        for n in range(64):
            for tile in range(4):
                part = pl.ds(128 * tile, 128)
                v = basis[i, n // 8, n % 8, :, part]
                term = v * v * inv_mult[pl.ds(8 * n, 8), part]
                totals[tile] = term if n == 0 else totals[tile] + term
        acc[2 * i] = (totals[0] + totals[1]) + (totals[2] + totals[3])

    def power(i, block):
        lane = pl.ds(256 * block, 256)
        mix = mix_ref[0:1, lane]

        def stage(h):
            rows = pl.ds(256 * h, 256)
            k = kap[rows, lane]
            k1 = k * grad[0, rows, lane]
            k2 = k * grad[1, rows, lane]
            flux[0, rows] = k1 + mix * k2
            h2, l2 = cut(k2 + mix * k1)
            h3, l3 = cut(k * grad[2, rows, lane])
            return jnp.concatenate([h2, h3, h2, h3, l2, l3], 0)

        staged = [stage(h) for h in range(2)]
        for h in range(2):
            value = dot(bwd_st[...], staged[h])
            ysum[pl.ds(256 * h, 256), lane] = value
            if h == 0:
                flux[1 + spare, 0:8, 0:128] = value[0:8, 0:128]
                for s in range(8):
                    for tile in range(2):
                        part = pl.ds(128 * tile, 128)
                        out = along(deriv.T, [flux[0, pl.ds(64 * r + 8 * s, 8), part] for r in range(8)])
                        for r in range(8):
                            flux[0, pl.ds(64 * r + 8 * s, 8), part] = out[r]
        total = None
        for h in range(2):
            rows = pl.ds(256 * h, 256)
            field = basis[i, 4 * h : 4 * h + 4, :, :, lane].reshape(256, 256)
            v = volume_ref[rows] * (0.05 / SCALE)
            value = ysum[rows, lane] + flux[0, rows] + jnp.concatenate([v, v], 1) * field
            basis[i + 1, 4 * h : 4 * h + 4, :, :, lane] = value.reshape(4, 8, 8, 256)
            part = fold(value * field)
            total = part if total is None else total + part
        return total

    for load in loads[10:13]:
        load.wait()
    finish_sides(0)
    gradient(0, 1)
    finish_edges(0)
    gradient(0, 0)
    moves[1].wait()
    moves[2].wait()
    kap[...] += place(jnp.concatenate([got_pack[1], got_pack[2]], 1))
    moves[0].wait()
    last_part = place(got_pack[0])
    for tile in range(4):
        lane = pl.ds(128 * tile, 128)
        kap[:, lane] = (
            volume_ref[...]
            * (kap[:, lane] + last_part[:, 128 * tile : 128 * tile + 128])
            * damping[tile]
        )

    def body(i, carry):
        ends = power(i, 0)
        start_ends(i + 1)
        acc[2 * i + 1] = ends + power(i, 1)
        start_middle(i + 1)
        norm(i)
        finish_sides(i + 1)
        gradient(i + 1, 1)
        finish_edges(i + 1)
        gradient(i + 1, 0)
        return carry

    lax.fori_loop(0, ITERS - 1, body, 0)

    final = ITERS - 1
    norm(final)
    totals = [None] * 4
    twice = [2.0 * mix_ref[:, pl.ds(128 * tile, 128)] for tile in range(4)]
    for n in range(64):
        eight = pl.ds(8 * n, 8)
        v5 = volume_ref[eight, :] * (0.05 / SCALE)
        for tile in range(4):
            part = pl.ds(128 * tile, 128)
            g1, g2, g3 = grad[0, eight, part], grad[1, eight, part], grad[2, eight, part]
            v = basis[final, n // 8, n % 8, :, part]
            term = kap[eight, part] * (g1 * (g1 + twice[tile] * g2) + (g2 * g2 + g3 * g3)) + v5 * (v * v)
            totals[tile] = term if n == 0 else totals[tile] + term
    acc[2 * final + 1] = (totals[0] + totals[1]) + (totals[2] + totals[3])

    rows = [jnp.sum(acc[k], axis=0, keepdims=True) for k in range(2 * ITERS)]
    rows = jnp.concatenate(rows + [jnp.zeros((6, 128), F32)], 0)
    mine = jnp.sum(rows, axis=1, keepdims=True)
    message = jnp.sum(jnp.where(iota((16, 128), 0) == iota((16, 128), 1), mine, 0.0), axis=0, keepdims=True)

    def everyone(message, sums, me, count, sends, recvs, peer):
        sums[me] = message
        copies = [
            pltpu.make_async_remote_copy(
                src_ref=sums.at[me],
                dst_ref=sums.at[me],
                send_sem=sends.at[j],
                recv_sem=recvs.at[j],
                device_id=peer(lax.rem(me + j, count)),
                device_id_type=MESH,
            )
            for j in range(1, count)
        ]
        for copy in copies:
            copy.start()
        for copy in copies:
            copy.wait()
        total = sums[0]
        for j in range(1, count):
            total = total + sums[j]
        return total

    message = everyone(message, chan_sum, chan, n_chan, chan_send, chan_recv, lambda c: (slab, c))
    message = everyone(message, slab_sum, slab, n_slab, slab_send, slab_recv, lambda s: (s, chan))
    lane1 = iota((1, 128), 1)
    moment = [
        jnp.sum(jnp.where(lane1 == k, message, 0.0), axis=1, keepdims=True) for k in range(2 * ITERS)
    ]
    weight = [w * (1.0 / SCALE) for w in krylov_weights(moment)]
    full = [jnp.broadcast_to(w, (8, 128)) for w in weight]
    for r in range(8):
        for s in range(8):
            for l in range(2):
                pieces = []
                for m in range(2):
                    total = full[0] * basis[0, r, s, :, lanes(m, l)]
                    for i in range(1, ITERS):
                        total = total + full[i] * basis[i, r, s, :, lanes(m, l)]
                    pieces.append(total)
                for h, total in enumerate(ends_middle(*pieces)):
                    out_ref[pl.ds(256 * r + 32 * s + 2 * h + l, 8, stride=4), :] = total


def flush_kernel(new_ref, out_ref, new_hbm, out_hbm, sem):
    first = pltpu.make_async_copy(new_ref, new_hbm, sem.at[0])
    second = pltpu.make_async_copy(out_ref, out_hbm, sem.at[1])
    first.start()
    second.start()
    first.wait()
    second.wait()


def step(u, index, prev, source, flags, plies, ops):
    n_slab, n_chan = lax.axis_size("slab"), lax.axis_size("chan")
    anywhere = pl.BlockSpec(memory_space=pl.ANY)
    vmem = pl.BlockSpec(memory_space=pltpu.VMEM)
    dma = pltpu.SemaphoreType.DMA
    new, warmth = pl.pallas_call(
        functools.partial(kernel, n_slab, n_chan),
        in_specs=[anywhere] * 11,
        out_specs=[vmem, vmem],
        out_shape=[
            pltpu.MemorySpace.VMEM((192, 8, 512), BF16),
            pltpu.MemorySpace.VMEM((2048, 128), F32),
        ],
        scratch_shapes=[
            pltpu.VMEM((192, 8, 512), BF16),
            pltpu.VMEM((1, 512), jnp.int32),
            pltpu.VMEM((2048, 128), F32),
            pltpu.VMEM((2048, 128), F32),
            pltpu.VMEM((2, 256), jnp.int32),
            pltpu.VMEM((2, 256), jnp.int32),
            pltpu.VMEM((512, 768), BF16),
            pltpu.VMEM((256, 1536), BF16),
            pltpu.VMEM((256, 256), BF16),
            pltpu.VMEM((512, 256), BF16),
            pltpu.VMEM((512, 128), F32),
            pltpu.VMEM((3, 3, 512, 512), F32),
            pltpu.VMEM((3, 512, 512), F32),
            pltpu.VMEM((528, 512), BF16),
            pltpu.VMEM((528, 256), BF16),
            pltpu.VMEM((3, 528, 128), BF16),
            pltpu.VMEM((3, 528, 128), BF16),
            pltpu.VMEM((ITERS + 1, 8, 8, 8, 512), F32),
            pltpu.VMEM((512, 512), F32),
            pltpu.VMEM((8, 512), F32),
            pltpu.VMEM((512, 512), F32),
            pltpu.VMEM((3, 512, 512), F32),
            pltpu.VMEM((512, 512), F32),
            pltpu.VMEM((2, 512, 256), F32),
            pltpu.VMEM((2 * ITERS, 8, 128), F32),
            pltpu.VMEM((2, 2, 8, 128), F32),
            pltpu.VMEM((2, 6, 8, 128), F32),
            pltpu.VMEM((2, 2, 2, 8, 8, 128), F32),
            pltpu.VMEM((2, 2, 2, 8, 8, 128), F32),
            pltpu.VMEM((n_chan, 1, 128), F32),
            pltpu.VMEM((n_slab, 1, 128), F32),
            dma((14,)),
            dma((3,)),
            dma((3,)),
            dma((2, 10)),
            dma((2, 10)),
            dma((n_chan,)),
            dma((n_chan,)),
            dma((n_slab,)),
            dma((n_slab,)),
        ],
        compiler_params=pltpu.CompilerParams(
            collective_id=0, has_side_effects=True
        ),
        name="step",
    )(
        u,
        index,
        prev,
        source,
        flags,
        plies,
        ops["forward"],
        ops["backward"],
        ops["lap_st"],
        ops["both_r"],
        ops["volume"],
    )
    new, warmth = pl.pallas_call(
        flush_kernel,
        in_specs=[vmem, vmem],
        out_specs=[anywhere, anywhere],
        out_shape=[
            jax.ShapeDtypeStruct((192, 8, 512), BF16),
            jax.ShapeDtypeStruct((2048, 128), F32),
        ],
        scratch_shapes=[dma((2,))],
        name="flush",
    )(
        pltpu.with_memory_space_constraint(new, pltpu.VMEM),
        pltpu.with_memory_space_constraint(warmth, pltpu.VMEM),
    )
    return new, warmth


def lanes_first(x):
    return x.reshape(512, 2, 2, 128).transpose(0, 2, 1, 3).reshape(2048, 128)


def on_device(u, index, prev, source, flags, plies):
    ops = operators()
    stepped, warmth = step(
        u.reshape(192, 8, 512),
        index.reshape(1, 512),
        lanes_first(prev),
        lanes_first(source),
        flags,
        plies,
        ops,
    )
    warmth = warmth.reshape(512, 2, 2, 128).transpose(0, 2, 1, 3).reshape(8, 8, 8, 2, 256)
    return stepped.reshape(3, 8, 8, 8, 512), warmth


def solution(mesh):
    in_specs = (
        P(None, None, None, None, ("slab", "chan")),
        P(("slab", "chan")),
        P(None, None, None, "chan", "slab"),
        P(None, None, None, "chan", "slab"),
        P("chan", "slab"),
        P("chan", "slab"),
    )
    out_specs = (P(None, None, None, None, ("slab", "chan")), P(None, None, None, "chan", "slab"))
    return jax.shard_map(
        on_device, mesh=mesh, in_specs=in_specs, out_specs=out_specs, check_vma=False
    )
```

profile of v0, /device:TPU:0, one launch (start us, length us, event | category | flops | bytes accessed | tf_op | source)
XLA Modules:
  0.0 54.0 jit_solution(8043503335345034992)
XLA Ops:
  0.6 51.9 %step.1 = (bf16[192,8,512]{2,1,0:T(8,128)(2,1)S(1)}, f32[2048,128]{1,0:T(8,128)S(1)}) custom-call(bf16[192,8,512]{2,1,0:T(8,128)(2,1)} %bitcast.18, s32[1,512]{1,0:T(1,128)} %bitcast.21, f32[2048,128]{1,0:T(8,128)} %bitcast.19, f32[2048,128]{1,0:T(8,128)} %bitcast.20, s32[2,256]{1,0:T(2,128)} %flag_hbm.1, s32[2,256]{1,0:T(2,128)} %ply_hbm.1, ...), custom_call_target="tpu_custom_call" | custom-call | tf_op jit(solution)/shard_map/step/pallas_call | solution.py:704
  52.5 1.5 %flush.1 = (bf16[192,8,512]{2,1,0:T(8,128)(2,1)}, f32[2048,128]{1,0:T(8,128)}) custom-call(bf16[192,8,512]{2,1,0:T(8,128)(2,1)S(1)} %get-tuple-element.6.new_ref, f32[2048,128]{1,0:T(8,128)S(1)} %get-tuple-element.7.out_ref), custom_call_target="tpu_custom_call" | custom-call | tf_op jit(solution)/shard_map/flush/pallas_call | solution.py:771
where the time goes:
time: 54.1 us; the launch traced here: 54 us
  Pallas kernels  53.4 us (99%)
  between operations  0.64 us (1%)
    pallas_call x1, Pallas kernels, step(): pl.pallas_call(functools.partial(kernel, n_slab, n_chan), in_specs=[anywh...  51.9 us
    pallas_call x1, Pallas kernels, step(): pl.pallas_call(flush_kernel, in_specs=[vmem, vmem], out_specs=[anywhere,...  1.51 us

commit v1 on v0

--- a/solution.py
+++ b/solution.py
@@ -332,7 +332,7 @@
                     else:
                         cond[rows, part] = (1.0 + 0.5 * square).astype(BF16)
 
-    for load in loads[5:9]:
+    for load in loads[5:10]:
         load.wait()
     fluid(0)
 
@@ -437,29 +437,52 @@
                 basis[i, 7, :, :, lanes(m, l)] = (high[m] + more).reshape(8, 8, 128)
                 basis[i, 0, :, :, lanes(m, l)] = (low[m] + less).reshape(8, 8, 128)
 
+    deriv = gll()[0]
+
     def finish_edges(i):
         turn, edges, sides = halo_copies(i, True, ())
         arrive(edges)
         first = lane8 == 0
         last = lane8 == 127
 
-        def add(l, s, at, slot_left, slot_right, has):
+        def lines(at, slot_left, slot_right, has):
             left_ok = has_left if has is None else has_left & has
             right_ok = has_right if has is None else has_right & has
-            basis[i, 0, s, :, lanes(0, l)] += jnp.where(
-                first & left_ok, pltpu.roll(edge_in[turn, slot_left], (128 - at) % 128, 1), 0.0
+            return (
+                jnp.where(first & left_ok, pltpu.roll(edge_in[turn, slot_left], (128 - at) % 128, 1), 0.0),
+                jnp.where(last & right_ok, pltpu.roll(edge_in[turn, slot_right], (127 - at) % 128, 1), 0.0),
             )
-            basis[i, 7, s, :, lanes(0, l)] += jnp.where(
-                last & right_ok, pltpu.roll(edge_in[turn, slot_right], (127 - at) % 128, 1), 0.0
-            )
-
+
+        corner = {
+            (0, 0): lines(15, EDGES.index((1, 1)), EDGES.index((-1, 1)), has_under),
+            (1, 7): lines(0, EDGES.index((1, -1)), EDGES.index((-1, -1)), has_over),
+        }
+        slope = [jnp.where(last, float(deriv[r, 7]), float(deriv[r, 0])) for r in range(8)]
         for l in range(2):
+            starts, ends = [], []
             for s in range(8):
-                add(l, s, s + 8 * l, EDGES.index((1, 0)), EDGES.index((-1, 0)), None)
-        add(0, 0, 15, EDGES.index((1, 1)), EDGES.index((-1, 1)), has_under)
-        add(1, 7, 0, EDGES.index((1, -1)), EDGES.index((-1, -1)), has_over)
-
-    loads[9].wait()
+                low, high = lines(s + 8 * l, EDGES.index((1, 0)), EDGES.index((-1, 0)), None)
+                if (l, s) in corner:
+                    low, high = low + corner[l, s][0], high + corner[l, s][1]
+                starts.append(low)
+                ends.append(high)
+                basis[i, 0, s, :, lanes(0, l)] += low
+                basis[i, 7, s, :, lanes(0, l)] += high
+                both = low + high
+                for r in range(8):
+                    grad[0, pl.ds(64 * r + 8 * s, 8), lanes(0, l)] += slope[r] * both
+            for r, face in ((0, along(deriv, starts)), (7, along(deriv, ends))):
+                for s in range(8):
+                    grad[1, pl.ds(64 * r + 8 * s, 8), lanes(0, l)] += face[s]
+        faces = jnp.concatenate(
+            [basis[i, r, :, :, 0:256].reshape(64, 256) for r in (0, 7)], 1
+        )
+        high, low = cut(faces)
+        main, rest = fwd_st[256:320, 0:64], fwd_st[256:320, 256:320]
+        value = dot(main, high) + (dot(rest, high) + dot(main, low))
+        grad[2, 0:64, 0:256] = value[:, :256]
+        grad[2, 448:512, 0:256] = value[:, 256:]
+
     fluid(1)
     pl.semaphore_wait(barrier, len(greet))
     start_ends(0)
@@ -516,7 +539,6 @@
             m_s = jnp.where(((at_s == 0) & (lateral > 0)) | ((at_s == 7) & (lateral < n_chan * 2 - 1)), 0.5, 1.0)
             inv_mult[:, lanes(m, l)] = m_r * m_s
 
-    deriv = gll()[0]
 
     spare = lax.div(slab, n_slab)
 
@@ -595,8 +617,8 @@
         load.wait()
     finish_sides(0)
     gradient(0, 1)
+    gradient(0, 0)
     finish_edges(0)
-    gradient(0, 0)
     moves[1].wait()
     moves[2].wait()
     kap[...] += place(jnp.concatenate([got_pack[1], got_pack[2]], 1))
@@ -618,8 +640,8 @@
         norm(i)
         finish_sides(i + 1)
         gradient(i + 1, 1)
+        gradient(i + 1, 0)
         finish_edges(i + 1)
-        gradient(i + 1, 0)
         return carry
 
     lax.fori_loop(0, ITERS - 1, body, 0)

time: 54.1 us -> 54.7 us (1.011)
    pallas_call x1, Pallas kernels: 51.9 us -> 52.4 us  [step(): pl.pallas_call(functools.partial(kernel, n_slab, n_chan), in_specs=[anywh...]
where the time goes in v1:
time: 54.7 us; the launch traced here: 54.6 us
  Pallas kernels  53.9 us (99%)
  between operations  0.64 us (1%)
    pallas_call x1, Pallas kernels, step(): pl.pallas_call(functools.partial(kernel, n_slab, n_chan), in_specs=[anywh...  52.4 us
    pallas_call x1, Pallas kernels, step(): pl.pallas_call(flush_kernel, in_specs=[vmem, vmem], out_specs=[anywhere,...  1.51 us

profile of v1, /device:TPU:0, one launch (start us, length us, event | category | flops | bytes accessed | tf_op | source)
XLA Modules:
  0.0 54.6 jit_solution(1227042435644659122)
XLA Ops:
  0.6 52.4 %step.1 = (bf16[192,8,512]{2,1,0:T(8,128)(2,1)S(1)}, f32[2048,128]{1,0:T(8,128)S(1)}) custom-call(bf16[192,8,512]{2,1,0:T(8,128)(2,1)} %bitcast.18, s32[1,512]{1,0:T(1,128)} %bitcast.21, f32[2048,128]{1,0:T(8,128)} %bitcast.19, f32[2048,128]{1,0:T(8,128)} %bitcast.20, s32[2,256]{1,0:T(2,128)} %flag_hbm.1, s32[2,256]{1,0:T(2,128)} %ply_hbm.1, ...), custom_call_target="tpu_custom_call" | custom-call | tf_op jit(solution)/shard_map/step/pallas_call | solution.py:726
  53.1 1.5 %flush.1 = (bf16[192,8,512]{2,1,0:T(8,128)(2,1)}, f32[2048,128]{1,0:T(8,128)}) custom-call(bf16[192,8,512]{2,1,0:T(8,128)(2,1)S(1)} %get-tuple-element.6.new_ref, f32[2048,128]{1,0:T(8,128)S(1)} %get-tuple-element.7.out_ref), custom_call_target="tpu_custom_call" | custom-call | tf_op jit(solution)/shard_map/flush/pallas_call | solution.py:793

commit v2 on v1

--- a/solution.py
+++ b/solution.py
@@ -416,12 +416,7 @@
         between(i, 1, turn)
         send(sides)
 
-    def finish_sides(i):
-        turn, edges, sides = halo_copies(i, False, (0, 1))
-        arrive(sides)
-        for k, (has, s, l) in enumerate(((has_under, 0, 0), (has_over, 7, 1))):
-            for m in range(2):
-                basis[i, :, s, :, lanes(m, l)] += jnp.where(has, side_in[turn, k, m], 0.0)
+    def local_axial(i):
         j = iota((64, 128), 1)
         for l in range(2):
             high = [basis[i, 7, :, :, lanes(m, l)].reshape(64, 128) for m in range(2)]
@@ -439,8 +434,9 @@
 
     deriv = gll()[0]
 
-    def finish_edges(i):
-        turn, edges, sides = halo_copies(i, True, ())
+    def finish(i):
+        turn, edges, sides = halo_copies(i, True, (0, 1))
+        arrive(sides)
         arrive(edges)
         first = lane8 == 0
         last = lane8 == 127
@@ -453,17 +449,32 @@
                 jnp.where(last & right_ok, pltpu.roll(edge_in[turn, slot_right], (127 - at) % 128, 1), 0.0),
             )
 
-        corner = {
-            (0, 0): lines(15, EDGES.index((1, 1)), EDGES.index((-1, 1)), has_under),
-            (1, 7): lines(0, EDGES.index((1, -1)), EDGES.index((-1, -1)), has_over),
-        }
+        for k, (has, s, l, at, dc) in enumerate(((has_under, 0, 0, 15, 1), (has_over, 7, 1, 0, -1))):
+            face = [[jnp.where(has, side_in[turn, k, m, r], 0.0) for r in range(8)] for m in range(2)]
+            ahead = [pltpu.roll(face[m][0], 127, 1) for m in range(2)]
+            behind = [pltpu.roll(face[m][7], 1, 1) for m in range(2)]
+            low, high = lines(at, EDGES.index((1, dc)), EDGES.index((-1, dc)), has)
+            for m in range(2):
+                more = jnp.where(lane8 == 63, ahead[1 - m], ahead[m])
+                less = jnp.where(lane8 == 64, behind[1 - m], behind[m])
+                if m == 0:
+                    more = jnp.where(last, high, more)
+                    less = jnp.where(first, low, less)
+                face[m][7] = face[m][7] + more
+                face[m][0] = face[m][0] + less
+            for m in range(2):
+                swept = along(deriv, face[m])
+                for r in range(8):
+                    basis[i, r, s, :, lanes(m, l)] += face[m][r]
+                    grad[0, pl.ds(64 * r + 8 * s, 8), lanes(m, l)] += swept[r]
+                    for q in range(8):
+                        grad[1, pl.ds(64 * r + 8 * q, 8), lanes(m, l)] += float(deriv[q, s]) * face[m][r]
+
         slope = [jnp.where(last, float(deriv[r, 7]), float(deriv[r, 0])) for r in range(8)]
         for l in range(2):
             starts, ends = [], []
             for s in range(8):
                 low, high = lines(s + 8 * l, EDGES.index((1, 0)), EDGES.index((-1, 0)), None)
-                if (l, s) in corner:
-                    low, high = low + corner[l, s][0], high + corner[l, s][1]
                 starts.append(low)
                 ends.append(high)
                 basis[i, 0, s, :, lanes(0, l)] += low
@@ -471,22 +482,28 @@
                 both = low + high
                 for r in range(8):
                     grad[0, pl.ds(64 * r + 8 * s, 8), lanes(0, l)] += slope[r] * both
-            for r, face in ((0, along(deriv, starts)), (7, along(deriv, ends))):
+            for r, line in ((0, along(deriv, starts)), (7, along(deriv, ends))):
                 for s in range(8):
-                    grad[1, pl.ds(64 * r + 8 * s, 8), lanes(0, l)] += face[s]
-        faces = jnp.concatenate(
-            [basis[i, r, :, :, 0:256].reshape(64, 256) for r in (0, 7)], 1
-        )
-        high, low = cut(faces)
+                    grad[1, pl.ds(64 * r + 8 * s, 8), lanes(0, l)] += line[s]
+
+        pieces = [basis[i, r, :, :, 0:256].reshape(64, 256) for r in (0, 7)]
+        pieces += [basis[i, :, 7 * l, :, lanes(m, l)].reshape(64, 128) for l in range(2) for m in range(2)]
+        high, low = cut(jnp.concatenate(pieces, 1))
         main, rest = fwd_st[256:320, 0:64], fwd_st[256:320, 256:320]
         value = dot(main, high) + (dot(rest, high) + dot(main, low))
-        grad[2, 0:64, 0:256] = value[:, :256]
-        grad[2, 448:512, 0:256] = value[:, 256:]
+        grad[2, 0:64, 0:256] = value[:, 0:256]
+        grad[2, 448:512, 0:256] = value[:, 256:512]
+        for l in range(2):
+            for m in range(2):
+                start = 512 + 256 * l + 128 * m
+                for r in range(8):
+                    grad[2, pl.ds(64 * r + 56 * l, 8), lanes(m, l)] = value[8 * r : 8 * r + 8, start : start + 128]
 
     fluid(1)
     pl.semaphore_wait(barrier, len(greet))
     start_ends(0)
     start_middle(0)
+    local_axial(0)
 
     def packed(start, count):
         chosen = (iota((count, 512), 0) + start == position).astype(F32).astype(BF16)
@@ -615,10 +632,9 @@
 
     for load in loads[10:13]:
         load.wait()
-    finish_sides(0)
     gradient(0, 1)
     gradient(0, 0)
-    finish_edges(0)
+    finish(0)
     moves[1].wait()
     moves[2].wait()
     kap[...] += place(jnp.concatenate([got_pack[1], got_pack[2]], 1))
@@ -637,11 +653,11 @@
         start_ends(i + 1)
         acc[2 * i + 1] = ends + power(i, 1)
         start_middle(i + 1)
+        local_axial(i + 1)
         norm(i)
-        finish_sides(i + 1)
         gradient(i + 1, 1)
         gradient(i + 1, 0)
-        finish_edges(i + 1)
+        finish(i + 1)
         return carry
 
     lax.fori_loop(0, ITERS - 1, body, 0)

time: 54.7 us -> 52.7 us (0.963)
  Pallas kernels: 53.9 us -> 51.9 us
    pallas_call x1, Pallas kernels: 52.4 us -> 50.4 us  [step(): pl.pallas_call(functools.partial(kernel, n_slab, n_chan), in_specs=[anywh...]
where the time goes in v2:
time: 52.7 us; the launch traced here: 52.6 us
  Pallas kernels  51.9 us (98%)
  between operations  0.64 us (1%)
    pallas_call x1, Pallas kernels, step(): pl.pallas_call(functools.partial(kernel, n_slab, n_chan), in_specs=[anywh...  50.4 us
    pallas_call x1, Pallas kernels, step(): pl.pallas_call(flush_kernel, in_specs=[vmem, vmem], out_specs=[anywhere,...  1.51 us

profile of v2, /device:TPU:0, one launch (start us, length us, event | category | flops | bytes accessed | tf_op | source)
XLA Modules:
  0.0 52.6 jit_solution(858343614374179909)
XLA Ops:
  0.6 50.4 %step.1 = (bf16[192,8,512]{2,1,0:T(8,128)(2,1)S(1)}, f32[2048,128]{1,0:T(8,128)S(1)}) custom-call(bf16[192,8,512]{2,1,0:T(8,128)(2,1)} %bitcast.18, s32[1,512]{1,0:T(1,128)} %bitcast.21, f32[2048,128]{1,0:T(8,128)} %bitcast.19, f32[2048,128]{1,0:T(8,128)} %bitcast.20, s32[2,256]{1,0:T(2,128)} %flag_hbm.1, s32[2,256]{1,0:T(2,128)} %ply_hbm.1, ...), custom_call_target="tpu_custom_call" | custom-call | tf_op jit(solution)/shard_map/step/pallas_call | solution.py:742
  51.1 1.5 %flush.1 = (bf16[192,8,512]{2,1,0:T(8,128)(2,1)}, f32[2048,128]{1,0:T(8,128)}) custom-call(bf16[192,8,512]{2,1,0:T(8,128)(2,1)S(1)} %get-tuple-element.6.new_ref, f32[2048,128]{1,0:T(8,128)S(1)} %get-tuple-element.7.out_ref), custom_call_target="tpu_custom_call" | custom-call | tf_op jit(solution)/shard_map/flush/pallas_call | solution.py:809

commit v3 on v2

--- a/solution.py
+++ b/solution.py
@@ -239,7 +239,7 @@
         )
     ]
     loads[13].start()
-    for load in loads[:13]:
+    for load in loads[5:10] + loads[:5] + loads[10:13]:
         load.start()
 
     barrier = pltpu.get_barrier_semaphore()
@@ -269,30 +269,6 @@
         jnp.where(iota((16, 512), 0) == 1, slot & 31, 0),
     )
     cond[512:528] = code.astype(F32).astype(BF16)
-
-    for load in loads[:5]:
-        load.wait()
-    for l in range(2):
-        halves = []
-        for h in range(2):
-            rows = pl.ds(2 * h + l, 512, stride=4)
-            halves.append(volume_ref[...] * (0.05 * prev_ref[rows, :] + source_ref[rows, :]))
-        for m, value in enumerate(ends_middle(*halves)):
-            basis[0, :, :, :, pl.ds(256 * m + 128 * l, 128)] = value.reshape(8, 8, 8, 128)
-    damping = []
-    mixing = []
-    for l in range(2):
-        flag = flag_ref[pl.ds(l, 1)]
-        ply = ply_ref[pl.ds(l, 1)].astype(F32)
-        damp = jnp.where(flag == 1, 1.0 / (1.0 + 0.25 * ply), 1.0) * (1.0 / SCALE)
-        mix = 0.4 * flag.astype(F32) * ply / (ply + 1.0)
-        wide = [jnp.broadcast_to(x, (8, 256)) for x in (damp, mix)]
-        damping.append(ends_middle(wide[0][:, :128], wide[0][:, 128:]))
-        mixing.append(ends_middle(wide[1][:, :128], wide[1][:, 128:]))
-    damping = [damping[l][m][0:1] for m in range(2) for l in range(2)]
-    mixing = [mixing[l][m] for m in range(2) for l in range(2)]
-    for tile in range(4):
-        mix_ref[:, pl.ds(128 * tile, 128)] = mixing[tile]
 
     def fluid(block):
         lane = pl.ds(256 * block, 256)
@@ -500,6 +476,31 @@
                     grad[2, pl.ds(64 * r + 56 * l, 8), lanes(m, l)] = value[8 * r : 8 * r + 8, start : start + 128]
 
     fluid(1)
+
+    for load in loads[:5]:
+        load.wait()
+    for l in range(2):
+        halves = []
+        for h in range(2):
+            rows = pl.ds(2 * h + l, 512, stride=4)
+            halves.append(volume_ref[...] * (0.05 * prev_ref[rows, :] + source_ref[rows, :]))
+        for m, value in enumerate(ends_middle(*halves)):
+            basis[0, :, :, :, pl.ds(256 * m + 128 * l, 128)] = value.reshape(8, 8, 8, 128)
+    damping = []
+    mixing = []
+    for l in range(2):
+        flag = flag_ref[pl.ds(l, 1)]
+        ply = ply_ref[pl.ds(l, 1)].astype(F32)
+        damp = jnp.where(flag == 1, 1.0 / (1.0 + 0.25 * ply), 1.0) * (1.0 / SCALE)
+        mix = 0.4 * flag.astype(F32) * ply / (ply + 1.0)
+        wide = [jnp.broadcast_to(x, (8, 256)) for x in (damp, mix)]
+        damping.append(ends_middle(wide[0][:, :128], wide[0][:, 128:]))
+        mixing.append(ends_middle(wide[1][:, :128], wide[1][:, 128:]))
+    damping = [damping[l][m][0:1] for m in range(2) for l in range(2)]
+    mixing = [mixing[l][m] for m in range(2) for l in range(2)]
+    for tile in range(4):
+        mix_ref[:, pl.ds(128 * tile, 128)] = mixing[tile]
+
     pl.semaphore_wait(barrier, len(greet))
     start_ends(0)
     start_middle(0)

time: 52.7 us -> 52.1 us (0.989)
    pallas_call x1, Pallas kernels: 50.4 us -> 49.9 us  [step(): pl.pallas_call(functools.partial(kernel, n_slab, n_chan), in_specs=[anywh...]
where the time goes in v3:
time: 52.1 us; the launch traced here: 52 us
  Pallas kernels  51.4 us (99%)
  between operations  0.64 us (1%)
    pallas_call x1, Pallas kernels, step(): pl.pallas_call(functools.partial(kernel, n_slab, n_chan), in_specs=[anywh...  49.9 us
    pallas_call x1, Pallas kernels, step(): pl.pallas_call(flush_kernel, in_specs=[vmem, vmem], out_specs=[anywhere,...  1.51 us

profile of v3, /device:TPU:0, one launch (start us, length us, event | category | flops | bytes accessed | tf_op | source)
XLA Modules:
  0.0 52.0 jit_solution(17237708247183157593)
XLA Ops:
  0.6 49.9 %step.1 = (bf16[192,8,512]{2,1,0:T(8,128)(2,1)S(1)}, f32[2048,128]{1,0:T(8,128)S(1)}) custom-call(bf16[192,8,512]{2,1,0:T(8,128)(2,1)} %bitcast.18, s32[1,512]{1,0:T(1,128)} %bitcast.21, f32[2048,128]{1,0:T(8,128)} %bitcast.19, f32[2048,128]{1,0:T(8,128)} %bitcast.20, s32[2,256]{1,0:T(2,128)} %flag_hbm.1, s32[2,256]{1,0:T(2,128)} %ply_hbm.1, ...), custom_call_target="tpu_custom_call" | custom-call | tf_op jit(solution)/shard_map/step/pallas_call | solution.py:743
  50.5 1.5 %flush.1 = (bf16[192,8,512]{2,1,0:T(8,128)(2,1)}, f32[2048,128]{1,0:T(8,128)}) custom-call(bf16[192,8,512]{2,1,0:T(8,128)(2,1)S(1)} %get-tuple-element.6.new_ref, f32[2048,128]{1,0:T(8,128)S(1)} %get-tuple-element.7.out_ref), custom_call_target="tpu_custom_call" | custom-call | tf_op jit(solution)/shard_map/flush/pallas_call | solution.py:810
